TPU v7x, 256 devices: a whole 4x4x8 slice. The times are simulated.
256 devices in a mesh: row: 8 (over x, core), col: 32 (over y, z).
Axes of the slice: x: 4, y: 4, z: 8, core: 2. Of those that a mesh axis runs over, the one named last changes fastest.
Arguments:
- response: float32 [18432, 18432], P('row', 'col'), may hold values from 0.002 to 0.02
- tile_map: int32 [288, 288], P('row', 'col'), may hold values 0 or 1
- band_offsets: int32 [288, 2], P('row'), may hold values from -48 to 48, as said below
- prior_spectra: float32 [512, 18432], P(None, 'col'), may hold values from 0.5 to 2
- boot_counts: int32 [512, 18432], P('col', 'row'), may hold values from 0 to 3
- spectrum: float32 [18432], P('row'), may hold values from 5 to 50
Outputs:
- covariance: float32 [18432, 18432], P('row', 'col')
- unfolded: float32 [512, 18432], P(None, 'col')
Inputs may be any that keep to these rules, and one draw needn't show every extreme that they name: `band_offsets`: column 0 is at most 0 and column 1 at least 0; some tile row reaches -48 and some reaches 48.
All inputs are finite; a program needn't handle non-finite values. No bound on the sum of `tile_map` on one device may be relied on, other than what follows from the above.
Results may differ from a plain program's by a relative error of at most 0.0003.
Values sent between devices are 32-bit elements; how exact they have to be, the bound alone decides.
A program may use at most 64 MiB of HBM per device.

v0:
```python
import jax
import jax.numpy as jnp
from jax import lax
from jax.sharding import Mesh
from jax.sharding import PartitionSpec as P

COL = ("col_0", "col_1")


def own_rows_2(subtotal, axes):
    for axis in axes:
        subtotal = lax.psum_scatter(subtotal, axis, scatter_dimension=0, tiled=True)
    return subtotal


def in_one(arrays, axis):
    ends = [0]
    for a in arrays:
        ends.append(ends[-1] + a.size)
    subtotal = lax.psum(jnp.concatenate([a.ravel() for a in arrays]), axis)
    return tuple((subtotal[b:e].reshape(a.shape) for a, b, e in zip(arrays, ends, ends[1:])))


def laid_out(pieces, dim):
    dims = list(pieces.shape[1:])
    dims[dim] *= pieces.shape[0]
    return jnp.moveaxis(pieces, 0, dim).reshape(dims)


def gather_in_order(array, axes, turns):
    pieces = array[None]
    for k in turns:
        pieces = lax.all_gather(pieces, axes[k], axis=0, tiled=True)
    block = [lax.axis_size(axes[k]) for k in reversed(turns)]
    pieces = pieces.reshape(*block, *array.shape)
    turned = sorted(range(len(turns)), key=lambda place: turns[len(turns) - 1 - place])
    return pieces.transpose(*turned, *range(len(turns), pieces.ndim)).reshape(-1, *array.shape)


def whole_of(array, axes, turns, dim):
    return laid_out(gather_in_order(array, axes, turns), dim)


def on_device(response, tile_map, band_offsets, prior_spectra, boot_counts, spectrum):
    row_place = lax.axis_index("row")
    col_place = lax.axis_index(COL)
    tiles_down, tiles_across = tile_map.shape
    tile_size = response.shape[0] // tiles_down
    measured = row_place * tiles_down + jnp.arange(tiles_down, dtype=jnp.int32)[:, None]
    truth = col_place * tiles_across + jnp.arange(tiles_across, dtype=jnp.int32)[None, :]
    inside = (truth >= measured + band_offsets[:, 0:1]) & (truth <= measured + band_offsets[:, 1:2])
    kept = (truth == measured) | inside & (tile_map == 1)
    expanded = jnp.repeat(jnp.repeat(kept, tile_size, 0), tile_size, 1)
    masked = jnp.where(expanded, response, jnp.zeros_like(response))
    replicas = prior_spectra.shape[0]
    measured_bins = masked.shape[0]
    folded = own_rows_2(
        jnp.dot(
            prior_spectra,
            masked.T,
            precision=lax.Precision.HIGHEST,
            preferred_element_type=jnp.float32,
        ),
        COL,
    )
    ratios = boot_counts.astype(jnp.float32) * spectrum[None, :] / folded
    fragment = lax.all_gather(ratios, COL, axis=0, tiled=True)
    partial_value = jnp.dot(
        fragment, masked, precision=lax.Precision.HIGHEST, preferred_element_type=jnp.float32
    )
    column_sums = jnp.sum(masked, axis=0)
    summed, efficiency = in_one((partial_value, column_sums), "row")
    unfolded = prior_spectra * summed / efficiency[None, :]
    centred = unfolded - jnp.mean(unfolded, axis=0)[None, :]
    regrouped = lax.all_to_all(centred, COL, split_axis=0, concat_axis=1, tiled=True)
    own_rows = lax.dynamic_slice_in_dim(regrouped, row_place * measured_bins, measured_bins, 1)
    covariance = jnp.dot(
        whole_of(own_rows, COL, (0, 1), 0).T,
        centred,
        precision=lax.Precision.HIGHEST,
        preferred_element_type=jnp.float32,
    )
    return (covariance / (replicas - 1), unfolded)


def solution(mesh):
    torus = Mesh(mesh.devices.reshape(mesh.shape["row"], 4, 8), ("row", "col_0", "col_1"))
    return jax.shard_map(
        on_device,
        mesh=torus,
        in_specs=(
            P("row", COL),
            P("row", COL),
            P("row", None),
            P(None, COL),
            P(COL, "row"),
            P("row"),
        ),
        out_specs=(P("row", COL), P(None, COL)),
        check_vma=False,
    )
```

profile of v0, /device:TPU:1, one launch (start us, length us, event | category | flops | bytes accessed | tf_op | source)
XLA Modules:
  0.0 435.8 jit_solution(6520451407332182556)
XLA Ops:
  9.4 14.7 %convolution_bitcast_fusion = f32[512,2304]{0,1:T(8,128)} fusion(f32[512,576]{0,1:T(8,128)S(1)} %copy-done, pred[2304,576]{0,1:T(32,128)(4,1)S(1)} %bitcast.21, f32[2304,576]{0,1:T(8,128)} %param.6), kind=kOutput, calls=%fused_computation.1 | convolution fusion | flops 8155054080 | bytes 12533760 | tf_op jit(solution)/shard_map/dot_general | solution.py:58
  24.2 57.5 %reduce-scatter.5.cloned.1.call-done = f32[128,2304]{0,1:T(8,128)} async-done(((f32[512,2304]{0,1:T(8,128)}), f32[128,2304]{0,1:T(8,128)}) %reduce-scatter.5.cloned.1.call-update) | async-done | bytes 1179664 | tf_op jit(solution)/shard_map/reduce_scatter | solution.py:12
  81.7 2.7 copy.34
  84.5 35.1 %reduce-scatter.7.cloned.1.call-done = f32[16,2304]{1,0:T(8,128)} async-done(((f32[128,2304]{1,0:T(8,128)}), f32[16,2304]{1,0:T(8,128)}) %reduce-scatter.7.cloned.1.call-update) | async-done | bytes 147472 | tf_op jit(solution)/shard_map/reduce_scatter | solution.py:12
  119.5 1.6 multiply_divide_fusion.1
  121.4 3.3 fusion
  124.7 80.6 %all-gather.4.cloned.1.call-done = f32[512,2304]{1,0:T(8,128)} async-done(((f32[16,2304]{1,0:T(8,128)}), f32[512,2304]{1,0:T(8,128)}) %all-gather.4.cloned.1.call-update) | async-done | bytes 4718608 | tf_op jit(solution)/shard_map/all_gather | solution.py:67
  205.3 13.8 %fusion.1 = f32[512,576]{1,0:T(8,128)S(1)} fusion(f32[512,2304]{1,0:T(8,128)} %all-gather.4.cloned.1.call-done, pred[2304,576]{0,1:T(32,128)(4,1)S(1)} %bitcast.23, f32[2304,576]{0,1:T(8,128)} %param.6), kind=kOutput, calls=%fused_computation.4 | convolution fusion | flops 8155054080 | bytes 12533760 | tf_op jit(solution)/shard_map/dot_general | solution.py:68
  219.1 1.6 reshape.51
  220.7 2.5 pad_maximum_fusion
  223.6 66.6 %all-reduce.2.cloned.1.call-done = f32[295488]{0:T(1024)} async-done(((f32[295488]{0:T(1024)}), f32[295488]{0:T(1024)}) %all-reduce.2.cloned.1.call-update) | async-done | bytes 1181968 | tf_op jit(solution)/shard_map/psum | solution.py:20
  290.2 1.3 slice-done
  291.5 1.4 reshape.52
  292.9 1.5 fusion.4
  294.4 1.2 broadcast_subtract_fusion
  295.6 9.3 %all-to-all-start = ((f32[32,16,576]{2,1,0:T(8,128)}), f32[32,16,576]{2,1,0:T(8,128)S(1)}, u32[]{:S(2)}, u32[]{:S(2)}) async-start(f32[32,16,576]{2,1,0:T(8,128)} %bitcast.4), calls=%async_computation.1 | async-start | bytes 2621440 | tf_op jit(solution)/shard_map/all_to_all | solution.py:75
  305.0 27.2 %all-to-all-done = f32[32,16,576]{2,1,0:T(8,128)S(1)} async-done(((f32[32,16,576]{2,1,0:T(8,128)}), f32[32,16,576]{2,1,0:T(8,128)S(1)}, u32[]{:S(2)}, u32[]{:S(2)}) %all-to-all-start) | async-done | bytes 1179680 | tf_op jit(solution)/shard_map/all_to_all | solution.py:75
  332.1 1.5 copy.30
  333.6 1.9 all_to_all.17
  335.5 11.0 %all-gather = f32[64,2304]{1,0:T(8,128)} all-gather(f32[16,2304]{1,0:T(8,128)S(1)} %constant_dynamic-slice_fusion), channel_id=2, replica_groups=mesh['row'=8,'col_0'=4,'col_1'=8] {'col_0'}, dimensions={0}, use_global_device_ids=true | all-gather | bytes 737280 | tf_op jit(solution)/shard_map/all_gather | solution.py:33
  346.5 1.4 copy.32
  347.9 66.0 %all-gather.6.cloned.1.call-done = f32[32,16,2304]{2,1,0:T(8,128)} async-done(((f32[4,16,2304]{2,1,0:T(8,128)}), f32[32,16,2304]{2,1,0:T(8,128)}) %all-gather.6.cloned.1.call-update) | async-done | bytes 4718608 | tf_op jit(solution)/shard_map/all_gather | solution.py:33
  414.0 2.7 copy.31
  416.7 12.6 %convolution_multiply_fusion = f32[2304,576]{0,1:T(8,128)} fusion(f32[512,2304]{1,0:T(8,128)S(1)} %bitcast.24, f32[512,576]{1,0:T(8,128)} %broadcast_subtract_fusion), kind=kOutput, calls=%fused_computation | convolution fusion | flops 8155054080 | bytes 11206656 | tf_op jit(solution)/shard_map/dot_general | solution.py:77
  (31 shorter events, 3.1 us)
Async XLA Ops:
  7.2 2.3 copy-start
  7.2 74.6 %reduce-scatter.5.cloned.1.call-start = ((), (), s32[]{:S(2)}) async-start(), calls=%async_computation.3 | async-start | bytes 5898240 | tf_op jit(solution)/shard_map/reduce_scatter | solution.py:12
  24.2 95.4 %copy-start.2 = (s32[16,2304]{1,0:T(8,128)S(1)}, s32[16,2304]{1,0:T(8,128)}, u32[]{:S(2)}) copy-start(s32[16,2304]{1,0:T(8,128)} %param.10) | copy-start | bytes 442372
  24.2 95.4 %copy-start.3 = (f32[2304]{0:T(1024)S(1)}, f32[2304]{0:T(1024)}, u32[]{:S(2)}) copy-start(f32[2304]{0:T(1024)} %param.11) | copy-start | bytes 27652
  24.2 95.3 %reduce-scatter.7.cloned.1.call-start = ((), (), s32[]{:S(2)}) async-start(), calls=%async_computation.7 | async-start | bytes 1327104 | tf_op jit(solution)/shard_map/reduce_scatter | solution.py:12
  84.4 120.8 %all-gather.4.cloned.1.call-start = ((), (), s32[]{:S(2)}) async-start(), calls=%async_computation.4 | async-start | bytes 4866048 | tf_op jit(solution)/shard_map/all_gather | solution.py:67
  121.2 169.0 %all-reduce.2.cloned.1.call-start = ((), (), s32[]{:S(2)}) async-start(), calls=%async_computation.5 | async-start | bytes 2367488 | tf_op jit(solution)/shard_map/psum | solution.py:20
  220.7 2.5 copy-start.1
  290.2 1.3 slice-start
  291.5 1.4 slice-start.1
  295.6 36.5 %all-to-all-start = ((f32[32,16,576]{2,1,0:T(8,128)}), f32[32,16,576]{2,1,0:T(8,128)S(1)}, u32[]{:S(2)}, u32[]{:S(2)}) async-start(f32[32,16,576]{2,1,0:T(8,128)} %bitcast.4), calls=%async_computation.1 | async-start | bytes 2621440 | tf_op jit(solution)/shard_map/all_to_all | solution.py:75
  304.9 109.1 %all-gather.6.cloned.1.call-start = ((), (), s32[]{:S(2)}) async-start(), calls=%async_computation.6 | async-start | bytes 5308416 | tf_op jit(solution)/shard_map/all_gather | solution.py:33
Sparse Core Ops, SparseCore 0:
  24.3 57.4 reduce-scatter.4
  84.9 34.6 reduce-scatter.6
  122.7 82.5 all-gather.3
  223.3 66.8 all-reduce.1
  346.7 67.2 all-gather.5
where the time goes:
time: 436 us
  waiting for transfers between devices  333 us (76%)
  matrix products  41.1 us (9%)
  local copies, waits for them, and re-layouts  15.4 us (4%)
  between operations  13.9 us (3%)
  other arithmetic  11.6 us (3%)
  blocking collectives  11 us (3%)
  starting transfers between devices  9.69 us (2%)
    reduce_scatter x2, waiting for transfers between devices, own_rows_2(): subtotal = lax.psum_scatter(subtotal, axis, scatter_dimension=0, tiled=True)  92.6 us
    all_gather x1, waiting for transfers between devices, on_device(): fragment = lax.all_gather(ratios, COL, axis=0, tiled=True)  80.6 us
    psum x1, waiting for transfers between devices, in_one(): subtotal = lax.psum(jnp.concatenate([a.ravel() for a in arrays]), axis)  66.6 us
    all_gather x1, waiting for transfers between devices, gather_in_order(): pieces = lax.all_gather(pieces, axes[k], axis=0, tiled=True)  66 us
    all_to_all x1, waiting for transfers between devices, on_device(): lax.all_to_all(centred, COL, split_axis=0, concat_axis=1, tiled=True)  27.2 us
    dot_general x1, matrix products, on_device(): jnp.dot(prior_spectra, masked.T, precision=lax.Precision.HIGHEST, preferr...  14.7 us
    dot_general x1, matrix products, on_device(): jnp.dot(fragment, masked, precision=lax.Precision.HIGHEST, preferred_elem...  13.8 us
    dot_general x1, matrix products, on_device(): jnp.dot(whole_of(own_rows, COL, (0, 1), 0).T, centred, precision=lax.Prec...  12.6 us
  transfers between devices with their start and end apart: 6, of which 6 were waited for; matrix products, arithmetic and copies ran while one was open for 1% of the time, Pallas kernels for 0%

commit v1 on v0

--- a/solution.py
+++ b/solution.py
@@ -30,7 +30,9 @@
 def gather_in_order(array, axes, turns):
     pieces = array[None]
     for k in turns:
-        pieces = lax.all_gather(pieces, axes[k], axis=0, tiled=True)
+        pieces = jnp.concatenate(
+            lax.all_to_all(jnp.stack([pieces] * lax.axis_size(axes[k])), axes[k], 0, 0), axis=0
+        )
     block = [lax.axis_size(axes[k]) for k in reversed(turns)]
     pieces = pieces.reshape(*block, *array.shape)
     turned = sorted(range(len(turns)), key=lambda place: turns[len(turns) - 1 - place])

time: 436 us -> 491 us (1.13)
  the two profiles are of different devices: /device:TPU:1 before, /device:TPU:6 now
where the time goes in v1:
time: 491 us
  waiting for transfers between devices  379 us (77%)
  matrix products  41.1 us (8%)
  local copies, waits for them, and re-layouts  18.2 us (4%)
  starting transfers between devices  16.2 us (3%)
  between operations  13.9 us (3%)
  other arithmetic  11.6 us (2%)
  blocking collectives  10.8 us (2%)
    all_to_all x1, waiting for transfers between devices, gather_in_order(): lax.all_to_all(jnp.stack([pieces] * lax.axis_size(axes[k])), axes[k], 0, 0)  105 us
    reduce_scatter x2, waiting for transfers between devices, own_rows_2(): subtotal = lax.psum_scatter(subtotal, axis, scatter_dimension=0, tiled=True)  96.2 us
    all_gather x1, waiting for transfers between devices, on_device(): fragment = lax.all_gather(ratios, COL, axis=0, tiled=True)  79.8 us
    psum x1, waiting for transfers between devices, in_one(): subtotal = lax.psum(jnp.concatenate([a.ravel() for a in arrays]), axis)  62.9 us
    all_to_all x1, waiting for transfers between devices, on_device(): lax.all_to_all(centred, COL, split_axis=0, concat_axis=1, tiled=True)  34.7 us
    dot_general x1, matrix products, on_device(): jnp.dot(prior_spectra, masked.T, precision=lax.Precision.HIGHEST, preferr...  14.7 us
    dot_general x1, matrix products, on_device(): jnp.dot(fragment, masked, precision=lax.Precision.HIGHEST, preferred_elem...  13.8 us
    dot_general x1, matrix products, on_device(): jnp.dot(whole_of(own_rows, COL, (0, 1), 0).T, centred, precision=lax.Prec...  12.6 us
  transfers between devices with their start and end apart: 6, of which 6 were waited for; matrix products, arithmetic and copies ran while one was open for 1% of the time, Pallas kernels for 0%

profile of v1, /device:TPU:6, one launch (start us, length us, event | category | flops | bytes accessed | tf_op | source)
XLA Modules:
  0.0 490.6 jit_solution(2258369504108413627)
XLA Ops:
  9.4 14.7 %convolution_bitcast_fusion = f32[512,2304]{0,1:T(8,128)} fusion(f32[512,576]{0,1:T(8,128)S(1)} %copy-done, pred[2304,576]{0,1:T(32,128)(4,1)S(1)} %bitcast.20, f32[2304,576]{0,1:T(8,128)} %param.6), kind=kOutput, calls=%fused_computation.1 | convolution fusion | flops 8155054080 | bytes 12533760 | tf_op jit(solution)/shard_map/dot_general | solution.py:60
  24.2 56.7 %reduce-scatter.5.cloned.1.call-done = f32[128,2304]{0,1:T(8,128)} async-done(((f32[512,2304]{0,1:T(8,128)}), f32[128,2304]{0,1:T(8,128)}) %reduce-scatter.5.cloned.1.call-update) | async-done | bytes 1179664 | tf_op jit(solution)/shard_map/reduce_scatter | solution.py:12
  80.9 2.7 copy.34
  83.7 39.5 %reduce-scatter.7.cloned.1.call-done = f32[16,2304]{1,0:T(8,128)} async-done(((f32[128,2304]{1,0:T(8,128)}), f32[16,2304]{1,0:T(8,128)}) %reduce-scatter.7.cloned.1.call-update) | async-done | bytes 147472 | tf_op jit(solution)/shard_map/reduce_scatter | solution.py:12
  123.2 1.6 multiply_divide_fusion.1
  125.1 3.3 fusion
  128.3 79.8 %all-gather.2.cloned.1.call-done = f32[512,2304]{1,0:T(8,128)} async-done(((f32[16,2304]{1,0:T(8,128)}), f32[512,2304]{1,0:T(8,128)}) %all-gather.2.cloned.1.call-update) | async-done | bytes 4718608 | tf_op jit(solution)/shard_map/all_gather | solution.py:69
  208.1 13.8 %fusion.1 = f32[512,576]{1,0:T(8,128)S(1)} fusion(f32[512,2304]{1,0:T(8,128)} %all-gather.2.cloned.1.call-done, pred[2304,576]{0,1:T(32,128)(4,1)S(1)} %bitcast.22, f32[2304,576]{0,1:T(8,128)} %param.6), kind=kOutput, calls=%fused_computation.4 | convolution fusion | flops 8155054080 | bytes 12533760 | tf_op jit(solution)/shard_map/dot_general | solution.py:70
  221.9 1.6 reshape.52
  223.5 2.5 pad_maximum_fusion
  226.4 62.9 %all-reduce.2.cloned.1.call-done = f32[295488]{0:T(1024)} async-done(((f32[295488]{0:T(1024)}), f32[295488]{0:T(1024)}) %all-reduce.2.cloned.1.call-update) | async-done | bytes 1181968 | tf_op jit(solution)/shard_map/psum | solution.py:20
  290.6 1.4 reshape.53
  292.0 1.5 fusion.4
  294.7 9.9 %all-to-all-start = ((f32[32,16,576]{2,1,0:T(8,128)}), f32[32,16,576]{2,1,0:T(8,128)S(1)}, u32[]{:S(2)}, u32[]{:S(2)}) async-start(f32[32,16,576]{2,1,0:T(8,128)} %bitcast.4), calls=%async_computation.1 | async-start | bytes 2621440 | tf_op jit(solution)/shard_map/all_to_all | solution.py:77
  304.6 34.7 %all-to-all-done = f32[32,16,576]{2,1,0:T(8,128)S(1)} async-done(((f32[32,16,576]{2,1,0:T(8,128)}), f32[32,16,576]{2,1,0:T(8,128)S(1)}, u32[]{:S(2)}, u32[]{:S(2)}) %all-to-all-start) | async-done | bytes 1179680 | tf_op jit(solution)/shard_map/all_to_all | solution.py:77
  339.2 1.5 copy.30
  340.7 1.9 all_to_all.23
  342.7 10.8 %all_to_all.29 = f32[4,1,16,2304]{3,2,1,0:T(8,128)S(1)} all-to-all(f32[4,1,16,2304]{3,2,1,0:T(8,128)S(1)} %stack.6), channel_id=1, replica_groups=mesh['row'=8,'col_0'=4,'col_1'=8] {'col_0'}, dimensions={0} | all-to-all | bytes 1179648 | tf_op jit(solution)/shard_map/all_to_all | solution.py:34
  353.5 2.7 stack.7
  356.2 6.0 %all-to-all-start.2 = ((f32[8,4,16,2304]{3,2,1,0:T(8,128)}), f32[8,4,16,2304]{3,2,1,0:T(8,128)}, u32[]{:S(2)}, u32[]{:S(2)}) async-start(f32[8,4,16,2304]{3,2,1,0:T(8,128)} %stack.7), calls=%async_computation.3 | async-start | bytes 9437184 | tf_op jit(solution)/shard_map/all_to_all | solution.py:34
  362.2 1.4 copy.32
  363.6 105.2 %all-to-all-done.2 = f32[8,4,16,2304]{3,2,1,0:T(8,128)} async-done(((f32[8,4,16,2304]{3,2,1,0:T(8,128)}), f32[8,4,16,2304]{3,2,1,0:T(8,128)}, u32[]{:S(2)}, u32[]{:S(2)}) %all-to-all-start.2) | async-done | bytes 4718624 | tf_op jit(solution)/shard_map/all_to_all | solution.py:34
  468.8 2.7 copy.31
  471.5 12.6 %convolution_multiply_fusion = f32[2304,576]{0,1:T(8,128)} fusion(f32[512,2304]{1,0:T(8,128)S(1)} %bitcast.23, f32[512,576]{1,0:T(8,128)} %broadcast_subtract_fusion), kind=kOutput, calls=%fused_computation | convolution fusion | flops 8155054080 | bytes 11206656 | tf_op jit(solution)/shard_map/dot_general | solution.py:79
  (32 shorter events, 5.5 us)
Async XLA Ops:
  7.2 2.3 copy-start
  7.2 73.8 %reduce-scatter.5.cloned.1.call-start = ((), (), s32[]{:S(2)}) async-start(), calls=%async_computation.5 | async-start | bytes 5898240 | tf_op jit(solution)/shard_map/reduce_scatter | solution.py:12
  24.2 99.0 %copy-start.2 = (s32[16,2304]{1,0:T(8,128)S(1)}, s32[16,2304]{1,0:T(8,128)}, u32[]{:S(2)}) copy-start(s32[16,2304]{1,0:T(8,128)} %param.10) | copy-start | bytes 442372
  24.2 99.0 %copy-start.3 = (f32[2304]{0:T(1024)S(1)}, f32[2304]{0:T(1024)}, u32[]{:S(2)}) copy-start(f32[2304]{0:T(1024)} %param.11) | copy-start | bytes 27652
  24.2 99.0 %reduce-scatter.7.cloned.1.call-start = ((), (), s32[]{:S(2)}) async-start(), calls=%async_computation.8 | async-start | bytes 1327104 | tf_op jit(solution)/shard_map/reduce_scatter | solution.py:12
  83.6 124.5 %all-gather.2.cloned.1.call-start = ((), (), s32[]{:S(2)}) async-start(), calls=%async_computation.6 | async-start | bytes 4866048 | tf_op jit(solution)/shard_map/all_gather | solution.py:69
  124.8 164.5 %all-reduce.2.cloned.1.call-start = ((), (), s32[]{:S(2)}) async-start(), calls=%async_computation.7 | async-start | bytes 2367488 | tf_op jit(solution)/shard_map/psum | solution.py:20
  223.5 2.5 copy-start.1
  289.3 1.3 slice-start
  290.6 1.4 slice-start.1
  294.7 44.5 %all-to-all-start = ((f32[32,16,576]{2,1,0:T(8,128)}), f32[32,16,576]{2,1,0:T(8,128)S(1)}, u32[]{:S(2)}, u32[]{:S(2)}) async-start(f32[32,16,576]{2,1,0:T(8,128)} %bitcast.4), calls=%async_computation.1 | async-start | bytes 2621440 | tf_op jit(solution)/shard_map/all_to_all | solution.py:77
  356.2 112.6 %all-to-all-start.2 = ((f32[8,4,16,2304]{3,2,1,0:T(8,128)}), f32[8,4,16,2304]{3,2,1,0:T(8,128)}, u32[]{:S(2)}, u32[]{:S(2)}) async-start(f32[8,4,16,2304]{3,2,1,0:T(8,128)} %stack.7), calls=%async_computation.3 | async-start | bytes 9437184 | tf_op jit(solution)/shard_map/all_to_all | solution.py:34
Sparse Core Ops, SparseCore 0:
  24.3 56.5 reduce-scatter.4
  84.0 39.1 reduce-scatter.6
  126.4 81.6 all-gather.1
  226.1 63.1 all-reduce.1
